TPU v7x, 32 devices: a whole 2x2x4 slice. The times are simulated.
32 devices in a mesh: gx: 16 (over z, y, x), bl: 2 (over core).
Axes of the slice: x: 2, y: 2, z: 4, core: 2. Of those that a mesh axis runs over, the one named last changes fastest.
Arguments:
- voltages: bfloat16 [2, 1024, 71680], P('bl', 'gx'), may hold values from -10 to 10, as said below
- model_magnitude: float32 [16, 2048], P('gx'), may hold values from 0.06 to 0.25
- model_phase: float32 [16, 2048], P('gx'), may hold values from -3.140625 to 3.140625
Outputs:
- visibilities: bfloat16 [16, 2, 2048, 2048], P('gx', None, 'bl')
- gains: float32 [2, 2, 1024, 16], P(None, 'bl', 'gx')
Inputs may be any that keep to these rules, and one draw needn't show every extreme that they name: `voltages`: each input's sampled voltage stream.
All inputs are finite; a program needn't handle non-finite values.
Results may differ from a plain program's by a relative error of at most 0.0057.
Values may be sent and summed in bfloat16 or wider, within the bound.
A program may use at most 64 MiB of HBM per device.

v0:
```python
import math

import jax
import jax.numpy as jnp
from jax import lax
from jax.sharding import PartitionSpec as P

NFFT = 2048
TAPS = 4
ITERS = 4


epsilon = 1e-06


def window_table(tap_count, length):
    positions = jnp.arange(tap_count * length, dtype=jnp.float32)
    centre = (positions + 0.5) / length - tap_count / 2.0
    hann_taper = 0.5 - 0.5 * jnp.cos(2.0 * math.pi * (positions + 0.5) / (tap_count * length))
    return (jnp.sinc(centre) * hann_taper).reshape(tap_count, length)


def channel_table(channels, stride, length):
    bin_index = jnp.arange(channels, dtype=jnp.int32) * stride + (stride + 1) // 2
    sample_index = jnp.arange(length, dtype=jnp.int32)
    phase_index = bin_index[:, None] * sample_index[None, :] % length
    angles = phase_index.astype(jnp.float32) * (2.0 * math.pi / length)
    factor = 1.0 / math.sqrt(length)
    return jnp.stack([jnp.cos(angles) * factor, -jnp.sin(angles) * factor], axis=1)


def stack_left(row_block):
    real_part = row_block[:, 0]
    imag_part = row_block[:, 1]
    upper = jnp.concatenate([real_part, imag_part], axis=2)
    lower = jnp.concatenate([imag_part, -real_part], axis=2)
    return jnp.stack([upper, lower], axis=1)


def on_device(voltages, model_magnitude, model_phase):
    groups = lax.axis_size("gx")
    local_channels = model_magnitude.shape[0]
    channels = local_channels * groups
    inputs = model_magnitude.shape[1]
    half_rows = inputs // lax.axis_size("bl")
    owned_inputs = voltages.shape[1]
    frames_total = voltages.shape[2] // NFFT
    spectra = frames_total - TAPS + 1
    taps_window = window_table(TAPS, NFFT)
    blocks = voltages.reshape(owned_inputs, frames_total, NFFT)
    frames = blocks[:, 0:spectra, :].astype(jnp.float32) * taps_window[0]
    for tap_index in range(1, TAPS):
        frames = (
            frames
            + blocks[:, tap_index : tap_index + spectra, :].astype(jnp.float32)
            * taps_window[tap_index]
        )
    stride = NFFT // 2 // channels
    transform = channel_table(channels, stride, NFFT).reshape(2 * channels, NFFT)
    spectra_local = lax.dot_general(
        transform,
        frames.reshape(owned_inputs * spectra, NFFT),
        (((1,), (1,)), ((), ())),
        precision=lax.Precision.HIGHEST,
        preferred_element_type=jnp.float32,
    )
    spectra_local = spectra_local.reshape(channels, 2, owned_inputs, spectra).astype(jnp.bfloat16)
    tile_index = lax.axis_index("bl")
    row_start = tile_index * half_rows
    own_rows = lax.all_to_all(spectra_local, "gx", split_axis=0, concat_axis=2, tiled=True)
    left_side = stack_left(own_rows)
    portion = lax.all_gather(own_rows, "bl", axis=2, tiled=True)
    right_side = jnp.concatenate([portion[:, 0], portion[:, 1]], axis=2)
    block_power = jnp.einsum(
        "cohk,crk->cohr", left_side, right_side, preferred_element_type=jnp.float32
    )
    whole_inputs = portion
    cross_sum, whole_inputs = (block_power, whole_inputs)
    cross_power = cross_sum * (1.0 / spectra)
    model_real = model_magnitude * jnp.cos(model_phase)
    model_imag = model_magnitude * jnp.sin(model_phase)
    inverse_square = 1.0 / (model_magnitude * model_magnitude)
    highest = lax.Precision.HIGHEST
    dense_values = whole_inputs.astype(jnp.float32)
    diagonal = jnp.sum(dense_values * dense_values, axis=(1, 3)) * (1.0 / spectra)

    def apply_power(probe_real, probe_imag):
        inner_real = jnp.einsum(
            "cps,cp->cs", dense_values[:, 0], probe_real, precision=highest
        ) + jnp.einsum("cps,cp->cs", dense_values[:, 1], probe_imag, precision=highest)
        inner_imag = jnp.einsum(
            "cps,cp->cs", dense_values[:, 0], probe_imag, precision=highest
        ) - jnp.einsum("cps,cp->cs", dense_values[:, 1], probe_real, precision=highest)
        real_out = (
            jnp.einsum("cps,cs->cp", dense_values[:, 0], inner_real, precision=highest)
            - jnp.einsum("cps,cs->cp", dense_values[:, 1], inner_imag, precision=highest)
        ) * (1.0 / spectra) - diagonal * probe_real
        imag_out = (
            jnp.einsum("cps,cs->cp", dense_values[:, 0], inner_imag, precision=highest)
            + jnp.einsum("cps,cs->cp", dense_values[:, 1], inner_real, precision=highest)
        ) * (1.0 / spectra) - diagonal * probe_imag
        return (real_out, imag_out)

    def single_step(gain_real, gain_imag):
        probe_real = gain_real * model_real - gain_imag * model_imag
        probe_imag = gain_real * model_imag + gain_imag * model_real
        image_real, image_imag = apply_power(probe_real, probe_imag)
        energy = (
            jnp.sum(probe_real * probe_real + probe_imag * probe_imag, axis=1, keepdims=True)
            + epsilon
        )
        factor = inverse_square / energy
        fresh_real = (image_real * model_real + image_imag * model_imag) * factor
        fresh_imag = (image_imag * model_real - image_real * model_imag) * factor
        return (fresh_real, fresh_imag)

    def double_step(pair_index, current):
        first_real, first_imag = single_step(current[0], current[1])
        fresh_real, fresh_imag = single_step(first_real, first_imag)
        return ((fresh_real + first_real) * 0.5, (fresh_imag + first_imag) * 0.5)

    start_gains = (
        jnp.ones((local_channels, inputs), jnp.float32),
        jnp.zeros((local_channels, inputs), jnp.float32),
    )
    gain_real, gain_imag = lax.fori_loop(0, ITERS // 2, double_step, start_gains)
    gain_pair = jnp.stack([gain_real, gain_imag], axis=1)
    own_gains = lax.dynamic_slice_in_dim(gain_pair, row_start, half_rows, 2)
    everything = lax.all_gather(own_gains, "gx", axis=0, tiled=True)
    owned_start = lax.axis_index("gx") * owned_inputs
    owned_gains = lax.dynamic_slice_in_dim(everything, owned_start, owned_inputs, 2)
    gain_output = jnp.transpose(owned_gains, (1, 2, 0))[:, None]
    return (cross_power.astype(jnp.bfloat16), gain_output)


def solution(mesh):
    in_specs = (P("bl", "gx", None), P("gx", None), P("gx", None))
    out_specs = (P("gx", None, "bl", None), P(None, "bl", "gx", None))
    return jax.shard_map(
        on_device, mesh=mesh, in_specs=in_specs, out_specs=out_specs, check_vma=False
    )
```

profile of v0, /device:TPU:0, one launch (start us, length us, event | category | flops | bytes accessed | tf_op | source)
XLA Modules:
  0.0 154.2 jit_solution(15563663636319006111)
XLA Ops:
  0.8 11.6 %reshape.292 = bf16[64,35,2048]{2,1,0:T(8,128)(2,1)} reshape(bf16[1,64,71680]{2,1,0:T(8,128)(2,1)} %param.5) | data formatting | bytes 18350080 | tf_op jit(solution)/shard_map/reshape | solution.py:50
  12.5 0.6 cosine_multiply_fusion
  13.1 19.9 %multiply_add_fusion.2 = f32[64,32,2048]{2,1,0:T(8,128)S(1)} fusion(bf16[64,35,2048]{2,1,0:T(8,128)(2,1)} %reshape.292, f32[2048]{0:T(1024)S(1)} %get-tuple-element.133, f32[2048]{0:T(1024)S(1)} %get-tuple-element.134, f32[2048]{0:T(1024)S(1)} %get-tuple-element.135, f32[2048]{0:T(1024)S(1)} %get-tuple-element.132), kind=kLoop, calls=%fused_computation.90 | loop fusion | flops 46137344 | bytes 50364416 | tf_op jit(solution)/shard_map/add | solution.py:54
  33.0 26.1 %fusion.60 = bf16[16,2,64,32]{2,0,3,1:T(8,128)(2,1)S(1)} fusion(f32[64,32,2048]{2,1,0:T(8,128)S(1)} %multiply_add_fusion.2, f32[16,1,2048]{2,0,1:T(8,128)S(1)} %get-tuple-element.140, f32[16,1,2048]{2,0,1:T(8,128)S(1)} %get-tuple-element.139), kind=kOutput, calls=%fused_computation.92 | convolution fusion | flops 1610743808 | bytes 17170432 | tf_op jit(solution)/shard_map/dot_general | solution.py:60
  59.2 0.9 reshape.336
  60.1 8.3 %all-to-all-start = ((bf16[16,2,2048]{2,1,0:T(2,128)(2,1)}), bf16[16,2,2048]{2,1,0:T(2,128)(2,1)S(1)}, u32[]{:S(2)}, u32[]{:S(2)}) async-start(bf16[16,2,2048]{2,1,0:T(2,128)(2,1)} %reshape.336), calls=%async_computation | async-start | bytes 262144 | tf_op jit(solution)/shard_map/all_to_all | solution.py:70
  68.7 7.5 %all-to-all-done = bf16[16,2,2048]{2,1,0:T(2,128)(2,1)S(1)} async-done(((bf16[16,2,2048]{2,1,0:T(2,128)(2,1)}), bf16[16,2,2048]{2,1,0:T(2,128)(2,1)S(1)}, u32[]{:S(2)}, u32[]{:S(2)}) %all-to-all-start) | async-done | bytes 131104 | tf_op jit(solution)/shard_map/all_to_all | solution.py:70
  76.9 2.0 %all_gather.6 = bf16[1,2,2048,32]{2,3,1,0:T(8,128)(2,1)S(1)} all-gather(bf16[1,2,1024,32]{2,3,1,0:T(8,128)(2,1)S(1)} %all_to_all.16), channel_id=1, replica_groups=mesh['gx'=16,'bl'=2] {'bl'}, dimensions={2}, use_global_device_ids=true | all-gather | bytes 393216 | tf_op jit(solution)/shard_map/all_gather | solution.py:72
  79.4 30.8 %while.13 = (s32[]{:T(128)}, f32[1,2048]{1,0:T(1,128)S(1)}, f32[1,2048]{1,0:T(1,128)S(1)}, f32[1,2048]{1,0:T(1,128)S(1)}, f32[1,2048]{1,0:T(1,128)S(1)}, /*index...) while((s32[]{:T(128)}, f32[1,2048]{1,0:T(1,128)S(1)}, ...), condition=%wide.region_4.5_spmd.clone, body=%wide.region_1.4_spmd.clone.sunk | while | flops 12705923 | bytes 17259680 | solution.py:126
  79.6 0.6 add_reduce_fusion.4
  80.2 0.6 convolution_bitcast_fusion.13
  80.8 0.6 fusion.179
  81.5 0.9 fusion.181
  82.4 0.6 convolution_bitcast_fusion.12
  83.0 0.6 fusion.177
  83.7 0.9 fusion.182
  84.6 0.9 fusion.180
  85.6 0.9 fusion.178
  87.2 0.7 add_reduce_fusion.5
  87.8 0.6 convolution_bitcast_fusion.15
  88.5 0.6 fusion.185
  89.1 0.9 fusion.187
  90.0 0.6 convolution_bitcast_fusion.14
  90.7 0.6 fusion.183
  91.3 0.9 fusion.188
  92.2 0.9 fusion.186
  93.2 0.9 fusion.184
  94.9 0.6 add_reduce_fusion.4
  95.5 0.6 convolution_bitcast_fusion.13
  96.1 0.6 fusion.179
  96.7 0.9 fusion.181
  97.7 0.6 convolution_bitcast_fusion.12
  98.3 0.6 fusion.177
  98.9 0.9 fusion.182
  99.9 0.9 fusion.180
  100.8 0.9 fusion.178
  102.5 0.7 add_reduce_fusion.5
  103.1 0.6 convolution_bitcast_fusion.15
  103.7 0.6 fusion.185
  104.4 0.9 fusion.187
  105.3 0.6 convolution_bitcast_fusion.14
  105.9 0.6 fusion.183
  106.6 0.9 fusion.188
  107.5 0.9 fusion.186
  108.5 0.9 fusion.184
  110.2 37.5 %all_gather.7 = f32[16,2,1024]{2,1,0:T(2,128)S(1)} all-gather(f32[1,2,1024]{2,1,0:T(2,128)S(1)} %fusion.88), channel_id=1, replica_groups=mesh['gx'=16,'bl'=2] {'gx'}, dimensions={0}, use_global_device_ids=true | all-gather | bytes 139264 | tf_op jit(solution)/shard_map/all_gather | solution.py:129
  147.8 0.6 copy.16
  148.4 5.8 %fusion.59 = bf16[1,2,1024,2048]{3,2,1,0:T(8,128)(2,1)} fusion(bf16[1,1,1024,64]{2,3,1,0:T(8,128)(2,1)S(1)} %get-tuple-element.131, bf16[1,1,1024,64]{2,3,1,0:T(8,128)(2,1)S(1)} %get-tuple-element.130, bf16[1,2048,32]{1,2,0:T(8,128)(2,1)S(1)} %get-tuple-element.127, bf16[1,2048,32]{1,2,0:T(8,128)(2,1)S(1)} %get-tuple-element.126), kind=kOutput, calls=%fused_computation.91 | convolution fusion | flops 545914880 | bytes 8912896 | tf_op jit(solution)/shard_map/cohk,crk->cohr/dot_general | solution.py:74
  (34 shorter events, 1.9 us)
Async XLA Ops:
  33.0 35.5 %copy-start = (f32[1,2048]{1,0:T(1,128)S(1)}, f32[1,2048]{1,0:T(1,128)}, u32[]{:S(2)}) copy-start(f32[1,2048]{1,0:T(1,128)} %param.6) | copy-start | bytes 24580
  33.0 35.5 %copy-start.1 = (f32[1,2048]{1,0:T(1,128)S(1)}, f32[1,2048]{1,0:T(1,128)}, u32[]{:S(2)}) copy-start(f32[1,2048]{1,0:T(1,128)} %param.7) | copy-start | bytes 24580
  60.1 16.2 %all-to-all-start = ((bf16[16,2,2048]{2,1,0:T(2,128)(2,1)}), bf16[16,2,2048]{2,1,0:T(2,128)(2,1)S(1)}, u32[]{:S(2)}, u32[]{:S(2)}) async-start(bf16[16,2,2048]{2,1,0:T(2,128)(2,1)} %reshape.336), calls=%async_computation | async-start | bytes 262144 | tf_op jit(solution)/shard_map/all_to_all | solution.py:70
where the time goes:
time: 155 us; the launch traced here: 154 us
  matrix products  57 us (37%)
  blocking collectives  39.5 us (25%)
  other arithmetic  23.9 us (15%)
  local copies, waits for them, and re-layouts  14.3 us (9%)
  starting transfers between devices  8.35 us (5%)
  waiting for transfers between devices  7.5 us (5%)
  loops' own time  2.97 us (2%)
    all_gather x1, blocking collectives, on_device(): everything = lax.all_gather(own_gains, 'gx', axis=0, tiled=True)  37.5 us
    dot_general x1, matrix products, on_device(): lax.dot_general(transform, frames.reshape(owned_inputs * spectra, NFFT),...  26.1 us
    add x1, other arithmetic, on_device(): frames + blocks[:, tap_index:tap_index + spectra, :].astype(jnp.float32)...  19.9 us
    reshape x1, local copies, waits for them, and re-layouts, on_device(): blocks = voltages.reshape(owned_inputs, frames_total, NFFT)  11.6 us
    all_to_all x1, starting transfers between devices, on_device(): lax.all_to_all(spectra_local, 'gx', split_axis=0, concat_axis=2, tiled=True)  8.35 us
    all_to_all x1, waiting for transfers between devices, on_device(): lax.all_to_all(spectra_local, 'gx', split_axis=0, concat_axis=2, tiled=True)  7.5 us
    dot_general x1, matrix products, on_device(): jnp.einsum('cohk,crk->cohr', left_side, right_side, preferred_element_typ...  5.77 us
    dot_general x4, matrix products, apply_power(): jnp.einsum('cps,cs->cp', dense_values[:, 0], inner_real, precision=highest)  3.8 us
  transfers between devices with their start and end apart: 1, of which 1 were waited for; matrix products, arithmetic and copies ran while one was open for 0% of the time, Pallas kernels for 0%

commit v1 on v0

--- a/solution.py
+++ b/solution.py
@@ -2,12 +2,16 @@
 
 import jax
 import jax.numpy as jnp
+import numpy as np
 from jax import lax
+from jax.experimental import pallas as pl
+from jax.experimental.pallas import tpu as pltpu
 from jax.sharding import PartitionSpec as P
 
 NFFT = 2048
 TAPS = 4
 ITERS = 4
+LANES = 128
 
 
 epsilon = 1e-06
@@ -133,9 +137,366 @@
     return (cross_power.astype(jnp.bfloat16), gain_output)
 
 
+def filter_bank(channels, stride):
+    position = (np.arange(TAPS * NFFT) + 0.5).reshape(TAPS, NFFT)
+    taper = np.sinc(position / NFFT - TAPS / 2.0) * (
+        0.5 - 0.5 * np.cos(2.0 * math.pi * position / (TAPS * NFFT))
+    )
+    bins = np.arange(channels) * stride + (stride + 1) // 2
+    angle = (bins[:, None] * np.arange(NFFT)[None, :] % NFFT) * (2.0 * math.pi / NFFT)
+    waves = np.stack([np.cos(angle), -np.sin(angle)]) / math.sqrt(NFFT)
+    bank = (taper[:, None, None, :] * waves[None]).reshape(TAPS * 2 * channels, NFFT)
+    high = bank.astype(jnp.bfloat16)
+    low = (bank - high.astype(np.float64)).astype(jnp.bfloat16)
+    return np.concatenate([high, low], axis=0)
+
+
+def channelize(v_ref, bank_ref, mag_ref, phase_ref, msg_ref, mr_ref, mi_ref, y_ref, f_ref):
+    step = pl.program_id(0)
+    owned = v_ref.shape[1]
+    per_step = v_ref.shape[2] // NFFT
+    channels, _, pairs, _ = msg_ref.shape
+    rows = jnp.concatenate(
+        [v_ref[0, :, k * NFFT : (k + 1) * NFFT] for k in range(per_step)], axis=0
+    )
+    y = lax.dot_general(
+        bank_ref[...], rows, (((1,), (1,)), ((), ())), preferred_element_type=jnp.float32
+    )
+    half = y.shape[0] // 2
+    y = y[:half] + y[half:]
+    tiles = y.shape[1] // LANES
+    for k in range(tiles):
+        y_ref[step * tiles + k] = y[:, k * LANES : (k + 1) * LANES]
+
+    @pl.when(step == 0)
+    def _():
+        mr_ref[...] = mag_ref[...] * jnp.cos(phase_ref[...])
+        mi_ref[...] = mag_ref[...] * jnp.sin(phase_ref[...])
+
+    @pl.when(step == pl.num_programs(0) - 1)
+    def _():
+        group = 2 * channels
+        low = lax.broadcasted_iota(jnp.int32, (group, LANES), 1) < owned
+
+        def part(tap, tile):
+            return y_ref[tile, tap * group : (tap + 1) * group, :]
+
+        turned = pltpu.roll(part(1, 0) + part(3, 1), owned, 1)
+        for j in range(pairs):
+            following = pltpu.roll(part(1, j + 1) + part(3, j + 2), owned, 1)
+            total = part(0, j) + part(2, j + 1) + jnp.where(low, turned, following)
+            f_ref[pl.ds(j, group, stride=pairs), :] = total
+            turned = following
+        for r in range(2):
+            for c in range(channels):
+                start = (r * channels + c) * pairs
+                msg_ref[c, r] = f_ref[start : start + pairs, :].astype(jnp.bfloat16)
+
+
+def exchange(
+    msg_ref, mag_ref, mr_ref, mi_ref, right_ref, own_ref, gain_ref,
+    slots, dense, yr_ref, yi_ref, wr_ref, wi_ref, gr_ref, gi_ref, pack, landed,
+    send_sem, recv_sem, fsend_sem, frecv_sem, gsend_sem, grecv_sem, local_sem,
+):
+    groups = lax.axis_size("gx")
+    g = lax.axis_index("gx")
+    b = lax.axis_index("bl")
+    other = 1 - b
+    mesh_id = pl.DeviceIdType.MESH
+    pairs = msg_ref.shape[2]
+    spectra = 2 * pairs
+    tiles = dense.shape[0]
+    owned = LANES // 2
+
+    barrier = pltpu.get_barrier_semaphore()
+
+    def greet(k, carry):
+        pl.semaphore_signal(
+            barrier, inc=1, device_id=(lax.rem(g + k, groups), b), device_id_type=mesh_id
+        )
+        return carry
+
+    lax.fori_loop(1, groups, greet, 0)
+    pl.semaphore_signal(barrier, inc=1, device_id=(g, other), device_id_type=mesh_id)
+    pl.semaphore_wait(barrier, groups)
+
+    def spread(k, source):
+        peer = lax.rem(g + k, groups)
+        return pltpu.make_async_remote_copy(
+            src_ref=msg_ref.at[peer], dst_ref=slots.at[b, source],
+            send_sem=send_sem.at[k], recv_sem=recv_sem.at[k],
+            device_id=(peer, b), device_id_type=mesh_id,
+        )
+
+    def relay(k, side):
+        source = lax.rem(g + groups - k, groups)
+        return pltpu.make_async_remote_copy(
+            src_ref=slots.at[b, source], dst_ref=slots.at[side, source],
+            send_sem=fsend_sem.at[k], recv_sem=frecv_sem.at[k],
+            device_id=(g, other), device_id_type=mesh_id,
+        )
+
+    def start_spread(k, carry):
+        spread(k, g).start()
+        return carry
+
+    lax.fori_loop(1, groups, start_spread, 0)
+    mine = pltpu.make_async_copy(msg_ref.at[g], slots.at[b, g], local_sem)
+    mine.start()
+    mine.wait()
+    relay(0, b).start()
+
+    def pass_on(k, carry):
+        spread(k, lax.rem(g + groups - k, groups)).wait_recv()
+        relay(k, b).start()
+        return carry
+
+    lax.fori_loop(1, groups, pass_on, 0)
+
+    def collect(k, carry):
+        relay(k, other).wait_recv()
+        return carry
+
+    lax.fori_loop(0, groups, collect, 0)
+
+    low = lax.broadcasted_iota(jnp.int32, (pairs, LANES), 1) < owned
+    for side in range(2):
+        for t in range(groups // 2):
+            tile = side * (groups // 2) + t
+            for r in range(2):
+                first = slots[side, 2 * t, r].astype(jnp.float32)
+                second = slots[side, 2 * t + 1, r].astype(jnp.float32)
+                even = jnp.where(low, first, pltpu.roll(second, owned, 1))
+                odd = jnp.where(low, pltpu.roll(first, owned, 1), second)
+                both = jnp.concatenate([even, odd], axis=0)
+                dense[tile, r * spectra : (r + 1) * spectra, :] = both
+                right_ref[
+                    r * spectra : (r + 1) * spectra, tile * LANES : (tile + 1) * LANES
+                ] = both.astype(jnp.bfloat16)
+            diagonal = jnp.sum(dense[tile] * dense[tile], axis=0, keepdims=True)
+            wr_ref[tile : tile + 1, :] = diagonal
+    for t in range(groups // 2):
+        own_ref[t] = dense[b * (groups // 2) + t]
+
+    scale = 1.0 / spectra
+    diagonal = wr_ref[...] * scale
+    model_real = mr_ref[...]
+    model_imag = mi_ref[...]
+    magnitude = mag_ref[...]
+    inverse_square = 1.0 / (magnitude * magnitude)
+
+    def single_step(gain_real, gain_imag):
+        probe_real = gain_real * model_real - gain_imag * model_imag
+        probe_imag = gain_real * model_imag + gain_imag * model_real
+        yr_ref[...] = probe_real
+        yi_ref[...] = probe_imag
+        total_real = jnp.zeros((spectra, LANES), jnp.float32)
+        total_imag = jnp.zeros((spectra, LANES), jnp.float32)
+        for t in range(tiles):
+            re = dense[t, :spectra, :]
+            im = dense[t, spectra:, :]
+            yr = yr_ref[t : t + 1, :]
+            yi = yi_ref[t : t + 1, :]
+            total_real = total_real + (re * yr + im * yi)
+            total_imag = total_imag + (re * yi - im * yr)
+        inner_real = jnp.sum(total_real, axis=1, keepdims=True) * scale
+        inner_imag = jnp.sum(total_imag, axis=1, keepdims=True) * scale
+        inner_real = jnp.broadcast_to(inner_real, (spectra, LANES))
+        inner_imag = jnp.broadcast_to(inner_imag, (spectra, LANES))
+        for t in range(tiles):
+            re = dense[t, :spectra, :]
+            im = dense[t, spectra:, :]
+            wr_ref[t : t + 1, :] = jnp.sum(
+                re * inner_real - im * inner_imag, axis=0, keepdims=True
+            )
+            wi_ref[t : t + 1, :] = jnp.sum(
+                re * inner_imag + im * inner_real, axis=0, keepdims=True
+            )
+        image_real = wr_ref[...] - diagonal * probe_real
+        image_imag = wi_ref[...] - diagonal * probe_imag
+        energy = jnp.sum(
+            jnp.sum(probe_real * probe_real + probe_imag * probe_imag, axis=1, keepdims=True),
+            axis=0,
+            keepdims=True,
+        ) + epsilon
+        factor = inverse_square / energy
+        fresh_real = (image_real * model_real + image_imag * model_imag) * factor
+        fresh_imag = (image_imag * model_real - image_real * model_imag) * factor
+        return (fresh_real, fresh_imag)
+
+    def double_step(pair_index, current):
+        first_real, first_imag = single_step(current[0], current[1])
+        fresh_real, fresh_imag = single_step(first_real, first_imag)
+        return ((fresh_real + first_real) * 0.5, (fresh_imag + first_imag) * 0.5)
+
+    gain_real, gain_imag = lax.fori_loop(
+        0,
+        ITERS // 2,
+        double_step,
+        (jnp.ones((tiles, LANES), jnp.float32), jnp.zeros((tiles, LANES), jnp.float32)),
+    )
+    gr_ref[...] = gain_real
+    gi_ref[...] = gain_imag
+    half = groups // 2
+    own_real = gr_ref[pl.ds(pl.multiple_of(b * half, half), half), :]
+    own_imag = gi_ref[pl.ds(pl.multiple_of(b * half, half), half), :]
+    low = lax.broadcasted_iota(jnp.int32, (half, LANES), 1) < owned
+    even = jnp.where(low, own_real, pltpu.roll(own_imag, owned, 1))
+    odd = jnp.where(low, pltpu.roll(own_real, owned, 1), own_imag)
+    for t in range(half):
+        pack[2 * t] = even[t : t + 1, :]
+        pack[2 * t + 1] = odd[t : t + 1, :]
+
+    def hand_back(k, owner):
+        peer = lax.rem(g + k, groups)
+        return pltpu.make_async_remote_copy(
+            src_ref=pack.at[peer], dst_ref=landed.at[owner],
+            send_sem=gsend_sem.at[k], recv_sem=grecv_sem.at[k],
+            device_id=(peer, b), device_id_type=mesh_id,
+        )
+
+    def start_back(k, carry):
+        hand_back(k, g).start()
+        return carry
+
+    lax.fori_loop(1, groups, start_back, 0)
+    landed[g] = pack[g]
+
+    def drain(k, carry):
+        spread(k, g).wait_send()
+        relay(k, b).wait_send()
+        hand_back(k, g).wait_send()
+        hand_back(k, lax.rem(g + groups - k, groups)).wait_recv()
+        return carry
+
+    relay(0, b).wait_send()
+    lax.fori_loop(1, groups, drain, 0)
+    for c in range(groups):
+        gain_ref[c : c + 1, :] = landed[c]
+
+
+def correlate(own_ref, right_ref, out_ref, real_side, imag_side):
+    depth = right_ref.shape[0]
+    spectra = depth // 2
+
+    @pl.when(pl.program_id(0) == 0)
+    def _():
+        real_side[:depth, :] = right_ref[...]
+        real_side[depth:, :] = jnp.zeros_like(right_ref)
+        imag_side[:depth, :] = jnp.zeros_like(right_ref)
+        imag_side[depth:, :] = right_ref[...]
+
+    own = own_ref[0] * (1.0 / spectra)
+    left = jnp.concatenate([own, own[spectra:], -own[:spectra]], axis=0)
+    left = jnp.transpose(left).astype(jnp.bfloat16)
+    out_ref[0, 0] = jnp.dot(
+        left, real_side[...], preferred_element_type=jnp.float32
+    ).astype(jnp.bfloat16)
+    out_ref[0, 1] = jnp.dot(
+        left, imag_side[...], preferred_element_type=jnp.float32
+    ).astype(jnp.bfloat16)
+
+
+def on_device_tiled(voltages, model_magnitude, model_phase):
+    groups = lax.axis_size("gx")
+    inputs = model_magnitude.shape[1]
+    owned = voltages.shape[1]
+    frames_total = voltages.shape[2] // NFFT
+    spectra = frames_total - TAPS + 1
+    pairs = spectra // 2
+    per_step = 2 * LANES // owned
+    steps = -(-frames_total // per_step)
+    tiles = inputs // LANES
+    half = tiles // 2
+    bank = jnp.asarray(filter_bank(groups, NFFT // 2 // groups))
+    magnitude = model_magnitude.reshape(tiles, LANES)
+    phase = model_phase.reshape(tiles, LANES)
+    f32 = jnp.float32
+    whole = lambda i: (0, 0)
+    table = jax.ShapeDtypeStruct((tiles, LANES), f32)
+    table_spec = pl.BlockSpec((tiles, LANES), whole)
+    messages, model_real, model_imag = pl.pallas_call(
+        channelize,
+        grid=(steps,),
+        in_specs=[
+            pl.BlockSpec((1, owned, per_step * NFFT), lambda i: (0, 0, i)),
+            pl.BlockSpec(bank.shape, whole),
+            table_spec,
+            table_spec,
+        ],
+        out_specs=[
+            pl.BlockSpec((groups, 2, pairs, LANES), lambda i: (0, 0, 0, 0)),
+            table_spec,
+            table_spec,
+        ],
+        out_shape=[
+            jax.ShapeDtypeStruct((groups, 2, pairs, LANES), jnp.bfloat16),
+            table,
+            table,
+        ],
+        scratch_shapes=[
+            pltpu.VMEM((steps * 2, TAPS * 2 * groups, LANES), f32),
+            pltpu.VMEM((2 * groups * pairs, LANES), f32),
+        ],
+        compiler_params=pltpu.CompilerParams(dimension_semantics=("arbitrary",)),
+        name="channelize",
+    )(voltages, bank, magnitude, phase)
+    vmem = pl.BlockSpec(memory_space=pltpu.VMEM)
+    right, own, gains = pl.pallas_call(
+        exchange,
+        in_specs=[vmem] * 4,
+        out_specs=[vmem] * 3,
+        out_shape=[
+            jax.ShapeDtypeStruct((2 * spectra, inputs), jnp.bfloat16),
+            jax.ShapeDtypeStruct((half, 2 * spectra, LANES), f32),
+            jax.ShapeDtypeStruct((groups, LANES), f32),
+        ],
+        scratch_shapes=[
+            pltpu.VMEM((2, groups, 2, pairs, LANES), jnp.bfloat16),
+            pltpu.VMEM((tiles, 2 * spectra, LANES), f32),
+        ]
+        + [pltpu.VMEM((tiles, LANES), f32)] * 6
+        + [pltpu.VMEM((groups, 1, LANES), f32)] * 2
+        + [pltpu.SemaphoreType.DMA((groups,))] * 6
+        + [pltpu.SemaphoreType.DMA],
+        compiler_params=pltpu.CompilerParams(collective_id=0, has_side_effects=True),
+        name="exchange",
+    )(messages, magnitude, model_real, model_imag)
+    visibilities = pl.pallas_call(
+        correlate,
+        grid=(half,),
+        in_specs=[
+            pl.BlockSpec((1, 2 * spectra, LANES), lambda i: (i, 0, 0)),
+            pl.BlockSpec((2 * spectra, inputs), whole),
+        ],
+        out_specs=pl.BlockSpec((1, 2, LANES, inputs), lambda i: (0, 0, i, 0)),
+        out_shape=jax.ShapeDtypeStruct((1, 2, half * LANES, inputs), jnp.bfloat16),
+        scratch_shapes=[pltpu.VMEM((4 * spectra, inputs), jnp.bfloat16)] * 2,
+        compiler_params=pltpu.CompilerParams(dimension_semantics=("arbitrary",)),
+        name="correlate",
+    )(own, right)
+    gains = jnp.transpose(gains.reshape(groups, 2, owned), (1, 2, 0))[:, None]
+    return (visibilities, gains)
+
+
 def solution(mesh):
     in_specs = (P("bl", "gx", None), P("gx", None), P("gx", None))
     out_specs = (P("gx", None, "bl", None), P(None, "bl", "gx", None))
+
+    def body(voltages, model_magnitude, model_phase):
+        spectra = voltages.shape[2] // NFFT - TAPS + 1
+        groups = mesh.shape["gx"]
+        tiled = (
+            model_magnitude.shape[0] == 1
+            and 2 * voltages.shape[1] == LANES
+            and mesh.shape["bl"] == 2
+            and groups % 16 == 0
+            and spectra % 32 == 0
+            and spectra & (spectra - 1) == 0
+        )
+        run = on_device_tiled if tiled else on_device
+        return run(voltages, model_magnitude, model_phase)
+
     return jax.shard_map(
-        on_device, mesh=mesh, in_specs=in_specs, out_specs=out_specs, check_vma=False
-    )
+        body, mesh=mesh, in_specs=in_specs, out_specs=out_specs, check_vma=False
+    )

time: 155 us -> 41.3 us (0.27)
  matrix products: 57 us -> 0 us
  blocking collectives: 39.5 us -> 0 us
  Pallas kernels: 0 us -> 38.6 us
  other arithmetic: 23.9 us -> 0 us
  local copies, waits for them, and re-layouts: 14.3 us -> 1.38 us
  starting transfers between devices: 8.35 us -> 0 us
  waiting for transfers between devices: 7.5 us -> 0 us
  loops' own time: 2.97 us -> 0 us
    dot_general x34 -> x0, matrix products: 57 us -> none  [the longest x1 26.1 us: on_device(): lax.dot_general(transform, frames.reshape(owned_inputs * spectra, NFFT),...]
    all_gather x2 -> x0, blocking collectives: 39.5 us -> none  [the longest x1 37.5 us: on_device(): everything = lax.all_gather(own_gains, 'gx', axis=0, tiled=True)]
    pallas_call x0 -> x3, Pallas kernels: none -> 38.6 us  [the longest x1 21.1 us: on_device_tiled(): pl.pallas_call(exchange, in_specs=[vmem] * 4, out_specs=[vmem] * 3, out_s...]
    add x2 -> x0, other arithmetic: 19.9 us -> none  [the longest x1 19.9 us: on_device(): frames + blocks[:, tap_index:tap_index + spectra, :].astype(jnp.float32)...]
    reshape x1 -> x2, local copies, waits for them, and re-layouts: 11.6 us -> 1.38 us  [on_device_tiled(): gains = jnp.transpose(gains.reshape(groups, 2, owned), (1, 2, 0))[:, None]]
    all_to_all x1 -> x0, starting transfers between devices: 8.35 us -> none  [on_device(): lax.all_to_all(spectra_local, 'gx', split_axis=0, concat_axis=2, tiled=True)]
    all_to_all x1 -> x0, waiting for transfers between devices: 7.5 us -> none  [on_device(): lax.all_to_all(spectra_local, 'gx', split_axis=0, concat_axis=2, tiled=True)]
    another operation x1 -> x0, loops' own time: 2.97 us -> none  [on_device(): lax.fori_loop(0, ITERS // 2, double_step, start_gains)]
  transfers between devices with their start and end apart: 1 -> 0, of which waited for: 1 -> 0; matrix products, arithmetic and copies ran while one was open for 0% -> 0% of each run, Pallas kernels for 0% -> 0%
where the time goes in v1:
time: 41.3 us; the launch traced here: 40.6 us
  Pallas kernels  38.6 us (93%)
  local copies, waits for them, and re-layouts  1.38 us (3%)
  between operations  0.64 us (2%)
    pallas_call x1, Pallas kernels, on_device_tiled(): pl.pallas_call(exchange, in_specs=[vmem] * 4, out_specs=[vmem] * 3, out_s...  21.1 us
    pallas_call x1, Pallas kernels, on_device_tiled(): pl.pallas_call(channelize, grid=(steps,), in_specs=[pl.BlockSpec((1, owne...  9.86 us
    pallas_call x1, Pallas kernels, on_device_tiled(): pl.pallas_call(correlate, grid=(half,), in_specs=[pl.BlockSpec((1, 2 * sp...  7.64 us
    reshape x2, local copies, waits for them, and re-layouts, on_device_tiled(): gains = jnp.transpose(gains.reshape(groups, 2, owned), (1, 2, 0))[:, None]  1.38 us

profile of v1, /device:TPU:0, one launch (start us, length us, event | category | flops | bytes accessed | tf_op | source)
XLA Modules:
  0.0 40.6 jit_solution(10984769854831006089)
XLA Ops:
  0.6 9.9 %channelize.1 = (bf16[16,2,16,128]{3,2,1,0:T(8,128)(2,1)}, f32[16,128]{1,0:T(8,128)}, f32[16,128]{1,0:T(8,128)}) custom-call(bf16[1,64,71680]{2,1,0:T(8,128)(2,1)} %v_ref.1, bf16[256,2048]{1,0:T(8,128)(2,1)} %constant.2.clone.bank_ref, f32[16,128]{1,0:T(8,128)} %bitcast.7, f32[16,128]{1,0:T(8,128)} %bitcast.10), custom_call_target="tpu_custom_call" | custom-call | tf_op jit(solution)/shard_map/channelize/pallas_call | solution.py:418
  10.5 21.1 %exchange.1 = (bf16[64,2048]{1,0:T(8,128)(2,1)}, f32[8,64,128]{2,1,0:T(8,128)}, f32[16,128]{1,0:T(8,128)}) custom-call(bf16[16,2,16,128]{3,2,1,0:T(8,128)(2,1)} %get-tuple-element.8.msg_ref, f32[16,128]{1,0:T(8,128)} %bitcast.8, f32[16,128]{1,0:T(8,128)} %get-tuple-element.9.mr_ref, f32[16,128]{1,0:T(8,128)} %get-tuple-element.10.mi_ref), custom_call_target="tpu_custom_call" | custom-call | tf_op jit(solution)/shard_map/exchange/pallas_call | solution.py:445
  31.6 7.6 %correlate.1 = bf16[1,2,1024,2048]{3,2,1,0:T(8,128)(2,1)} custom-call(f32[8,64,128]{2,1,0:T(8,128)} %get-tuple-element.11.own_ref, bf16[64,2048]{1,0:T(8,128)(2,1)} %get-tuple-element.12.right_ref), custom_call_target="tpu_custom_call" | custom-call | tf_op jit(solution)/shard_map/correlate/pallas_call | solution.py:465
  39.2 0.8 %reshape.15 = f32[16,2,64]{2,1,0:T(2,128)S(1)} reshape(f32[16,128]{1,0:T(8,128)} %get-tuple-element.13) | data formatting | bytes 16384 | tf_op jit(solution)/shard_map/reshape | solution.py:478
  40.0 0.6 %copy.8 = f32[16,2,64]{2,0,1:T(8,128)} copy(f32[16,2,64]{2,1,0:T(2,128)S(1)} %reshape.15) | data formatting | bytes 16384 | tf_op jit(solution)/shard_map/reshape | solution.py:478

commit v2 on v1

--- a/solution.py
+++ b/solution.py
@@ -148,7 +148,7 @@
     bank = (taper[:, None, None, :] * waves[None]).reshape(TAPS * 2 * channels, NFFT)
     high = bank.astype(jnp.bfloat16)
     low = (bank - high.astype(np.float64)).astype(jnp.bfloat16)
-    return np.concatenate([high, low], axis=0)
+    return np.concatenate([high, low], axis=0).T
 
 
 def channelize(v_ref, bank_ref, mag_ref, phase_ref, msg_ref, mr_ref, mi_ref, y_ref, f_ref):
@@ -159,14 +159,12 @@
     rows = jnp.concatenate(
         [v_ref[0, :, k * NFFT : (k + 1) * NFFT] for k in range(per_step)], axis=0
     )
-    y = lax.dot_general(
-        bank_ref[...], rows, (((1,), (1,)), ((), ())), preferred_element_type=jnp.float32
-    )
-    half = y.shape[0] // 2
-    y = y[:half] + y[half:]
-    tiles = y.shape[1] // LANES
+    y = jnp.dot(rows, bank_ref[...], preferred_element_type=jnp.float32)
+    half = y.shape[1] // 2
+    y = y[:, :half] + y[:, half:]
+    tiles = y.shape[0] // LANES
     for k in range(tiles):
-        y_ref[step * tiles + k] = y[:, k * LANES : (k + 1) * LANES]
+        y_ref[step * tiles + k] = jnp.transpose(y[k * LANES : (k + 1) * LANES])
 
     @pl.when(step == 0)
     def _():
@@ -208,17 +206,7 @@
     tiles = dense.shape[0]
     owned = LANES // 2
 
-    barrier = pltpu.get_barrier_semaphore()
-
-    def greet(k, carry):
-        pl.semaphore_signal(
-            barrier, inc=1, device_id=(lax.rem(g + k, groups), b), device_id_type=mesh_id
-        )
-        return carry
-
-    lax.fori_loop(1, groups, greet, 0)
-    pl.semaphore_signal(barrier, inc=1, device_id=(g, other), device_id_type=mesh_id)
-    pl.semaphore_wait(barrier, groups)
+    pl.semaphore_wait(pltpu.get_barrier_semaphore(), groups)
 
     def spread(k, source):
         peer = lax.rem(g + k, groups)
@@ -375,7 +363,40 @@
         gain_ref[c : c + 1, :] = landed[c]
 
 
-def correlate(own_ref, right_ref, out_ref, real_side, imag_side):
+def greet_all():
+    groups = lax.axis_size("gx")
+    g = lax.axis_index("gx")
+    b = lax.axis_index("bl")
+    other = 1 - b
+    mesh_id = pl.DeviceIdType.MESH
+    barrier = pltpu.get_barrier_semaphore()
+
+    def greet(k, carry):
+        pl.semaphore_signal(
+            barrier, inc=1, device_id=(lax.rem(g + k, groups), b), device_id_type=mesh_id
+        )
+        return carry
+
+    lax.fori_loop(1, groups, greet, 0)
+    pl.semaphore_signal(barrier, inc=1, device_id=(g, other), device_id_type=mesh_id)
+
+
+def fused(
+    v_ref, bank_ref, mag_ref, phase_ref, right_ref, own_ref, gain_ref,
+    msg_ref, mr_ref, mi_ref, y_ref, f_ref, *rest
+):
+    @pl.when(pl.program_id(0) == 0)
+    def _():
+        greet_all()
+
+    channelize(v_ref, bank_ref, mag_ref, phase_ref, msg_ref, mr_ref, mi_ref, y_ref, f_ref)
+
+    @pl.when(pl.program_id(0) == pl.num_programs(0) - 1)
+    def _():
+        exchange(msg_ref, mag_ref, mr_ref, mi_ref, right_ref, own_ref, gain_ref, *rest)
+
+
+def correlate(own_ref, right_ref, gain_ref, out_ref, owned_ref, real_side, imag_side):
     depth = right_ref.shape[0]
     spectra = depth // 2
 
@@ -385,10 +406,16 @@
         real_side[depth:, :] = jnp.zeros_like(right_ref)
         imag_side[:depth, :] = jnp.zeros_like(right_ref)
         imag_side[depth:, :] = right_ref[...]
-
-    own = own_ref[0] * (1.0 / spectra)
-    left = jnp.concatenate([own, own[spectra:], -own[:spectra]], axis=0)
-    left = jnp.transpose(left).astype(jnp.bfloat16)
+        owned = owned_ref.shape[3]
+        owned_ref[0, 0] = gain_ref[:, :owned]
+        owned_ref[1, 0] = gain_ref[:, owned:]
+
+    parts = []
+    for t in range(own_ref.shape[0]):
+        own = own_ref[t] * (1.0 / spectra)
+        part = jnp.concatenate([own, own[spectra:], -own[:spectra]], axis=0)
+        parts.append(jnp.transpose(part).astype(jnp.bfloat16))
+    left = jnp.concatenate(parts, axis=0)
     out_ref[0, 0] = jnp.dot(
         left, real_side[...], preferred_element_type=jnp.float32
     ).astype(jnp.bfloat16)
@@ -404,7 +431,7 @@
     frames_total = voltages.shape[2] // NFFT
     spectra = frames_total - TAPS + 1
     pairs = spectra // 2
-    per_step = 2 * LANES // owned
+    per_step = 4 * LANES // owned
     steps = -(-frames_total // per_step)
     tiles = inputs // LANES
     half = tiles // 2
@@ -415,8 +442,8 @@
     whole = lambda i: (0, 0)
     table = jax.ShapeDtypeStruct((tiles, LANES), f32)
     table_spec = pl.BlockSpec((tiles, LANES), whole)
-    messages, model_real, model_imag = pl.pallas_call(
-        channelize,
+    right, own, gains = pl.pallas_call(
+        fused,
         grid=(steps,),
         in_specs=[
             pl.BlockSpec((1, owned, per_step * NFFT), lambda i: (0, 0, i)),
@@ -425,33 +452,21 @@
             table_spec,
         ],
         out_specs=[
-            pl.BlockSpec((groups, 2, pairs, LANES), lambda i: (0, 0, 0, 0)),
-            table_spec,
-            table_spec,
+            pl.BlockSpec((2 * spectra, inputs), whole),
+            pl.BlockSpec((half, 2 * spectra, LANES), lambda i: (0, 0, 0)),
+            pl.BlockSpec((groups, LANES), whole),
         ],
-        out_shape=[
-            jax.ShapeDtypeStruct((groups, 2, pairs, LANES), jnp.bfloat16),
-            table,
-            table,
-        ],
-        scratch_shapes=[
-            pltpu.VMEM((steps * 2, TAPS * 2 * groups, LANES), f32),
-            pltpu.VMEM((2 * groups * pairs, LANES), f32),
-        ],
-        compiler_params=pltpu.CompilerParams(dimension_semantics=("arbitrary",)),
-        name="channelize",
-    )(voltages, bank, magnitude, phase)
-    vmem = pl.BlockSpec(memory_space=pltpu.VMEM)
-    right, own, gains = pl.pallas_call(
-        exchange,
-        in_specs=[vmem] * 4,
-        out_specs=[vmem] * 3,
         out_shape=[
             jax.ShapeDtypeStruct((2 * spectra, inputs), jnp.bfloat16),
             jax.ShapeDtypeStruct((half, 2 * spectra, LANES), f32),
             jax.ShapeDtypeStruct((groups, LANES), f32),
         ],
         scratch_shapes=[
+            pltpu.VMEM((groups, 2, pairs, LANES), jnp.bfloat16),
+            pltpu.VMEM((tiles, LANES), f32),
+            pltpu.VMEM((tiles, LANES), f32),
+            pltpu.VMEM((steps * 4, TAPS * 2 * groups, LANES), f32),
+            pltpu.VMEM((2 * groups * pairs, LANES), f32),
             pltpu.VMEM((2, groups, 2, pairs, LANES), jnp.bfloat16),
             pltpu.VMEM((tiles, 2 * spectra, LANES), f32),
         ]
@@ -459,24 +474,33 @@
         + [pltpu.VMEM((groups, 1, LANES), f32)] * 2
         + [pltpu.SemaphoreType.DMA((groups,))] * 6
         + [pltpu.SemaphoreType.DMA],
-        compiler_params=pltpu.CompilerParams(collective_id=0, has_side_effects=True),
-        name="exchange",
-    )(messages, magnitude, model_real, model_imag)
-    visibilities = pl.pallas_call(
+        compiler_params=pltpu.CompilerParams(
+            dimension_semantics=("arbitrary",), collective_id=0, has_side_effects=True
+        ),
+        name="gather_solve",
+    )(voltages, bank, magnitude, phase)
+    batch = math.gcd(half, 4)
+    visibilities, gains = pl.pallas_call(
         correlate,
-        grid=(half,),
+        grid=(half // batch,),
         in_specs=[
-            pl.BlockSpec((1, 2 * spectra, LANES), lambda i: (i, 0, 0)),
+            pl.BlockSpec((batch, 2 * spectra, LANES), lambda i: (i, 0, 0)),
             pl.BlockSpec((2 * spectra, inputs), whole),
+            pl.BlockSpec((groups, LANES), whole),
         ],
-        out_specs=pl.BlockSpec((1, 2, LANES, inputs), lambda i: (0, 0, i, 0)),
-        out_shape=jax.ShapeDtypeStruct((1, 2, half * LANES, inputs), jnp.bfloat16),
+        out_specs=[
+            pl.BlockSpec((1, 2, batch * LANES, inputs), lambda i: (0, 0, i, 0)),
+            pl.BlockSpec((2, 1, groups, owned), lambda i: (0, 0, 0, 0)),
+        ],
+        out_shape=[
+            jax.ShapeDtypeStruct((1, 2, half * LANES, inputs), jnp.bfloat16),
+            jax.ShapeDtypeStruct((2, 1, groups, owned), f32),
+        ],
         scratch_shapes=[pltpu.VMEM((4 * spectra, inputs), jnp.bfloat16)] * 2,
         compiler_params=pltpu.CompilerParams(dimension_semantics=("arbitrary",)),
         name="correlate",
-    )(own, right)
-    gains = jnp.transpose(gains.reshape(groups, 2, owned), (1, 2, 0))[:, None]
-    return (visibilities, gains)
+    )(own, right, gains)
+    return (visibilities, jnp.swapaxes(gains, 2, 3))
 
 
 def solution(mesh):

time: 41.3 us -> 30 us (0.73); the launches traced: 40.6 us -> 29.8 us
  Pallas kernels: 38.6 us -> 29.1 us
  local copies, waits for them, and re-layouts: 1.38 us -> 0 us
    pallas_call x3 -> x2, Pallas kernels: 38.6 us -> 29.1 us  [the longest x1 23.3 us: on_device_tiled(): pl.pallas_call(fused, grid=(steps,), in_specs=[pl.BlockSpec((1, owned, pe...]
    reshape x2 -> x0, local copies, waits for them, and re-layouts: 1.38 us -> none  [on_device_tiled(): gains = jnp.transpose(gains.reshape(groups, 2, owned), (1, 2, 0))[:, None]]
where the time goes in v2:
time: 30 us; the launch traced here: 29.8 us
  Pallas kernels  29.1 us (97%)
  between operations  0.64 us (2%)
    pallas_call x1, Pallas kernels, on_device_tiled(): pl.pallas_call(fused, grid=(steps,), in_specs=[pl.BlockSpec((1, owned, pe...  23.3 us
    pallas_call x1, Pallas kernels, on_device_tiled(): pl.pallas_call(correlate, grid=(half // batch,), in_specs=[pl.BlockSpec((...  5.81 us

profile of v2, /device:TPU:0, one launch (start us, length us, event | category | flops | bytes accessed | tf_op | source)
XLA Modules:
  0.0 29.8 jit_solution(4894394678114354178)
XLA Ops:
  0.6 23.3 %gather_solve.1 = (bf16[64,2048]{1,0:T(8,128)(2,1)}, f32[8,64,128]{2,1,0:T(8,128)}, f32[16,128]{1,0:T(8,128)}) custom-call(bf16[1,64,71680]{2,1,0:T(8,128)(2,1)} %v_ref.1, bf16[2048,256]{1,0:T(8,128)(2,1)} %constant.2.clone.bank_ref, f32[16,128]{1,0:T(8,128)} %bitcast.3, f32[16,128]{1,0:T(8,128)} %bitcast.4), custom_call_target="tpu_custom_call" | custom-call | tf_op jit(solution)/shard_map/gather_solve/pallas_call | solution.py:445
  24.0 5.8 %correlate.1 = (bf16[1,2,1024,2048]{3,2,1,0:T(8,128)(2,1)}, f32[2,1,16,64]{3,2,1,0:T(8,128)}) custom-call(f32[8,64,128]{2,1,0:T(8,128)} %get-tuple-element.7.own_ref, bf16[64,2048]{1,0:T(8,128)(2,1)} %get-tuple-element.8.right_ref, f32[16,128]{1,0:T(8,128)} %get-tuple-element.9.gain_ref), custom_call_target="tpu_custom_call" | custom-call | tf_op jit(solution)/shard_map/correlate/pallas_call | solution.py:483
